TPU v7x, 32 devices: a whole 2x2x4 slice. The times are simulated.
32 devices in a mesh: sector: 4 (over z), group: 8 (over y, x, core).
Axes of the slice: x: 2, y: 2, z: 4, core: 2. Of those that a mesh axis runs over, the one named last changes fastest.
Arguments:
- spectrum: float32 [1152, 128, 512], P('group', None, 'sector'), may hold values from 0.1 to 2
- land_mask: int32 [128, 512], P(None, 'sector'), may hold values 0 or 1
- wind_field: float32 [2, 128, 512], P(None, 'group', 'sector'), may hold values from -3 to 3
- assignment: int32 [1152], replicated, may hold values from 0 to 1151, each once
- courant: float32 [32], replicated, may hold values from 0.3 to 0.65
- growth: float32 [32], replicated, may hold values from 0.1 to 0.5
- whitecap: float32 [32], replicated, may hold values from 0.2 to 1
- weights: float32 [32], replicated, may hold values from 0.5 to 5
- spread: float32 [32, 36, 36], replicated, may hold values from -1 to 1
Outputs:
- updated: float32 [1152, 128, 512], P('group', None, 'sector')
Inputs may be any that keep to these rules, and one draw needn't show every extreme that they name: `assignment`: each component number appears exactly once.
All inputs are finite; a program needn't handle non-finite values. No bound on the sum of `land_mask` on one device may be relied on, other than what follows from the above.
Results may differ from a plain program's by a relative error of at most 0.00007.
Values sent between devices are 32-bit elements; how exact they have to be, the bound alone decides.
No kernel may reach another device: no remote copies, remote signals or barrier semaphores. Data moves between devices by JAX's collectives and lax.ppermute only.
A program may use at most 128 MiB of HBM per device.

v0:
```python
import math
import jax
import jax.numpy as jnp
from jax import lax
from jax.sharding import PartitionSpec as P

DIRS = 36
FREQ = 32
SUBSTEPS = 6
LAT = 128


def extended(cells, sides, width):
    for axis, dim in sides:
        count = lax.axis_size(axis)
        head = lax.slice_in_dim(cells, 0, width, axis=dim)
        tail = lax.slice_in_dim(cells, cells.shape[dim] - width, cells.shape[dim], axis=dim)
        cells = jnp.concatenate(
            [
                lax.ppermute(tail, axis, [(i, (i + 1) % count) for i in range(count)]),
                cells,
                lax.ppermute(head, axis, [((i + 1) % count, i) for i in range(count)]),
            ],
            axis=dim,
        )
    return cells


def freq_onehot(frequency):
    return (frequency[:, None] == jnp.arange(FREQ)[None, :]).astype(jnp.float32)


def flow_terms(kinds, courant):
    direction = kinds % DIRS
    frequency = kinds // DIRS
    angles = (direction.astype(jnp.float32) + 0.5) * (2.0 * math.pi / DIRS)
    speeds = jnp.dot(freq_onehot(frequency), courant, precision=lax.Precision.HIGHEST)
    latitude = (jnp.arange(LAT).astype(jnp.float32) + 0.5 - LAT / 2) * (math.pi / 2160.0)
    flow_x = speeds[:, None] * jnp.cos(angles)[:, None] / jnp.cos(latitude)[None, :]
    flow_y = speeds * jnp.sin(angles)
    return (flow_x, flow_y)


def combine(centre, from_west, from_east, rates):
    keep_rate, east_rate, west_rate, north_rate, south_rate = rates
    from_south = jnp.pad(centre[:, :-1], ((0, 0), (1, 0), (0, 0)))
    from_north = jnp.pad(centre[:, 1:], ((0, 0), (0, 1), (0, 0)))
    return (
        keep_rate * centre
        + east_rate * from_west
        + west_rate * from_east
        + north_rate * from_south
        + south_rate * from_north
    )


def propagate(wave, flow_x, flow_y, sea_mask):
    rates = (
        1.0 - jnp.abs(flow_x)[:, :, None] - jnp.abs(flow_y)[:, None, None],
        jnp.maximum(flow_x, 0.0)[:, :, None],
        jnp.maximum(-flow_x, 0.0)[:, :, None],
        jnp.maximum(flow_y, 0.0)[:, None, None],
        jnp.maximum(-flow_y, 0.0)[:, None, None],
    )
    for substep in range(SUBSTEPS):
        padded = extended(wave, (("sector", 2),), 1)
        wave = combine(wave, padded[:, :, :-2], padded[:, :, 2:], rates) * sea_mask[None]
    return wave


def local(spectrum, land_mask, wind_field, assignment, courant, growth, whitecap, weights, spread):
    member = lax.axis_index("group")
    comps_dev = spectrum.shape[0]
    lon_local = spectrum.shape[2]
    all_comps = assignment.shape[0]
    rows_dev = wind_field.shape[1]
    sea_mask = land_mask.astype(jnp.float32)
    kinds = lax.dynamic_slice_in_dim(assignment, member * comps_dev, comps_dev, 0)
    flow_x, flow_y = flow_terms(kinds, courant)
    moved = lax.all_to_all(
        propagate(spectrum, flow_x, flow_y, sea_mask),
        "group",
        split_axis=1,
        concat_axis=0,
        tiled=True,
    )
    points = rows_dev * lon_local
    energy = moved.reshape(all_comps, points)
    sea_rows = lax.dynamic_slice_in_dim(sea_mask, member * rows_dev, rows_dev, 0).reshape(points)
    winds = wind_field.reshape(2, points)
    direction = assignment % DIRS
    frequency = assignment // DIRS
    angles = (direction.astype(jnp.float32) + 0.5) * (2.0 * math.pi / DIRS)
    per_freq = jnp.stack((growth, whitecap, weights), axis=1)
    picked = jnp.dot(freq_onehot(frequency), per_freq, precision=lax.Precision.HIGHEST)
    kind_onehot = (assignment[:, None] == jnp.arange(all_comps)[None, :]).astype(jnp.float32)
    picked_rows = jnp.dot(
        kind_onehot, spread.reshape(FREQ * DIRS, DIRS), precision=lax.Precision.HIGHEST
    )
    dir_onehot = (jnp.arange(DIRS)[:, None] == direction[None, :]).astype(jnp.float32)
    same_freq = (frequency[:, None] == frequency[None, :]).astype(jnp.float32)
    coupling = jnp.dot(picked_rows, dir_onehot, precision=lax.Precision.HIGHEST) * same_freq
    loading = jnp.sum(picked[:, 2][:, None] * energy, axis=0) / all_comps
    drive = (
        jnp.cos(angles)[:, None] * winds[0][None, :] + jnp.sin(angles)[:, None] * winds[1][None, :]
    )
    exponent = (
        picked[:, 0][:, None] * jnp.maximum(drive, 0.0)
        - picked[:, 1][:, None] * (loading / (1.0 + loading))[None, :]
    )
    mixed = jnp.dot(coupling, energy, precision=lax.Precision.HIGHEST)
    renewed = (energy * jnp.exp(exponent) + 0.5 * mixed) * sea_rows[None, :]
    return lax.all_to_all(
        renewed.reshape(all_comps, rows_dev, lon_local),
        "group",
        split_axis=0,
        concat_axis=1,
        tiled=True,
    )


def solution(mesh):
    in_specs = (
        P("group", None, "sector"),
        P(None, "sector"),
        P(None, "group", "sector"),
        P(),
        P(),
        P(),
        P(),
        P(),
        P(),
    )
    out_specs = P("group", None, "sector")
    return jax.shard_map(local, mesh=mesh, in_specs=in_specs, out_specs=out_specs, check_vma=False)
```

profile of v0, /device:TPU:0, one launch (start us, length us, event | category | flops | bytes accessed | tf_op | source)
XLA Modules:
  0.0 494.8 jit_solution(8796984362894581755)
XLA Ops:
  0.0 9.6 %copy.15 = f32[144,128,128]{1,0,2:T(8,128)} copy(f32[144,128,128]{2,1,0:T(8,128)} %param.9) | data formatting | bytes 18874368 | tf_op args[0]
  9.6 0.9 fusion.83
  10.5 3.1 collective-permute-start
  13.6 2.1 collective-permute-start.1
  15.8 14.2 %fusion.82 = (f32[144,127,128]{1,0,2:T(8,128)}, f32[144,127,128]{1,0,2:T(8,128)}) fusion(f32[144,128,128]{1,0,2:T(8,128)} %copy.15), kind=kLoop, calls=%fused_computation.122 | loop fusion | bytes 37453824 | tf_op jit(solution)/shard_map/slice | solution.py:46
  30.0 0.1 and_select_fusion.1
  30.1 0.2 fusion.55
  30.3 0.2 fusion.70
  30.6 0.1 subtract_subtract_fusion
  30.7 0.1 copy.22
  30.8 16.4 %fusion.43 = f32[144,128,128]{1,0,2:T(8,128)S(1)} fusion(f32[144,128,1]{1,0,2:T(8,128)S(1)} %collective-permute-done.1, f32[144,128,128]{1,0,2:T(8,128)} %copy.15, f32[144,128,1]{1,0,2:T(8,128)S(1)} %collective-permute-done, f32[144,127,128]{1,0,2:T(8,128)} %get-tuple-element.31, f32[144,127,128]{1,0,2:T(8,128)} %get-tuple-element.30, ...), kind=kLoop, calls=%fused_computation.57 | loop fusion | flops 28311552 | bytes 38036608 | tf_op jit(solution)/shard_map/mul | solution.py:67
  47.2 0.1 collective-permute-start.2
  47.3 3.8 collective-permute-start.3
  51.1 8.1 %fusion.80 = (f32[144,127,128]{1,0,2:T(8,128)}, f32[144,127,128]{1,0,2:T(8,128)}) fusion(f32[144,128,128]{1,0,2:T(8,128)S(1)} %fusion.43), kind=kLoop, calls=%fused_computation.120 | loop fusion | bytes 37453824 | tf_op jit(solution)/shard_map/slice | solution.py:46
  59.2 13.2 %fusion.36 = f32[144,128,128]{1,0,2:T(8,128)} fusion(f32[144,128,1]{1,0,2:T(8,128)S(1)} %collective-permute-done.3, f32[144,128,128]{1,0,2:T(8,128)S(1)} %fusion.43, f32[144,128,1]{1,0,2:T(8,128)S(1)} %collective-permute-done.2, f32[144,127,128]{1,0,2:T(8,128)} %get-tuple-element.27, f32[144,127,128]{1,0,2:T(8,128)} %get-tuple-element.26, ...), kind=kLoop, calls=%fused_computation.48 | loop fusion | flops 28311552 | bytes 38036608 | tf_op jit(solution)/shard_map/mul | solution.py:67
  72.4 0.9 fusion.79
  73.3 0.1 collective-permute-start.4
  73.4 3.8 collective-permute-start.5
  77.2 14.4 %fusion.78 = (f32[144,127,128]{1,0,2:T(8,128)}, f32[144,127,128]{1,0,2:T(8,128)}) fusion(f32[144,128,128]{1,0,2:T(8,128)} %fusion.36), kind=kLoop, calls=%fused_computation.118 | loop fusion | bytes 37453824 | tf_op jit(solution)/shard_map/slice | solution.py:46
  91.7 13.2 %fusion.29 = f32[144,128,128]{1,0,2:T(8,128)} fusion(f32[144,128,1]{1,0,2:T(8,128)S(1)} %collective-permute-done.5, f32[144,128,128]{1,0,2:T(8,128)S(1)} %bitcast.47, f32[144,128,1]{1,0,2:T(8,128)S(1)} %collective-permute-done.4, f32[144,127,128]{1,0,2:T(8,128)} %get-tuple-element.23, f32[144,127,128]{1,0,2:T(8,128)} %get-tuple-element.22, ...), kind=kLoop, calls=%fused_computation.39 | loop fusion | flops 28311552 | bytes 38036608 | tf_op jit(solution)/shard_map/mul | solution.py:67
  104.9 0.9 fusion.77
  105.8 0.1 collective-permute-start.6
  105.9 3.9 collective-permute-start.7
  109.9 14.4 %fusion.76 = (f32[144,127,128]{1,0,2:T(8,128)}, f32[144,127,128]{1,0,2:T(8,128)}) fusion(f32[144,128,128]{1,0,2:T(8,128)} %fusion.29), kind=kLoop, calls=%fused_computation.116 | loop fusion | bytes 37453824 | tf_op jit(solution)/shard_map/slice | solution.py:46
  124.3 13.2 %fusion.22 = f32[144,128,128]{1,0,2:T(8,128)} fusion(f32[144,128,1]{1,0,2:T(8,128)S(1)} %collective-permute-done.7, f32[144,128,128]{1,0,2:T(8,128)S(1)} %bitcast.49, f32[144,128,1]{1,0,2:T(8,128)S(1)} %collective-permute-done.6, f32[144,127,128]{1,0,2:T(8,128)} %get-tuple-element.19, f32[144,127,128]{1,0,2:T(8,128)} %get-tuple-element.18, ...), kind=kLoop, calls=%fused_computation.30 | loop fusion | flops 28311552 | bytes 38036608 | tf_op jit(solution)/shard_map/mul | solution.py:67
  137.5 0.9 fusion.75
  138.5 3.8 collective-permute-start.9
  142.3 14.4 %fusion.74 = (f32[144,127,128]{1,0,2:T(8,128)}, f32[144,127,128]{1,0,2:T(8,128)}) fusion(f32[144,128,128]{1,0,2:T(8,128)} %fusion.22), kind=kLoop, calls=%fused_computation.114 | loop fusion | bytes 37453824 | tf_op jit(solution)/shard_map/slice | solution.py:46
  156.8 16.4 %fusion.15 = f32[144,128,128]{1,0,2:T(8,128)S(1)} fusion(f32[144,128,1]{1,0,2:T(8,128)S(1)} %collective-permute-done.9, f32[144,128,128]{1,0,2:T(8,128)} %fusion.22, f32[144,128,1]{1,0,2:T(8,128)S(1)} %collective-permute-done.8, f32[144,127,128]{1,0,2:T(8,128)} %get-tuple-element.15, f32[144,127,128]{1,0,2:T(8,128)} %get-tuple-element.14, ...), kind=kLoop, calls=%fused_computation.21 | loop fusion | flops 28311552 | bytes 38036608 | tf_op jit(solution)/shard_map/mul | solution.py:67
  173.2 3.8 collective-permute-start.11
  177.1 8.1 %fusion.72 = (f32[144,127,128]{1,0,2:T(8,128)}, f32[144,127,128]{1,0,2:T(8,128)}) fusion(f32[144,128,128]{1,0,2:T(8,128)S(1)} %fusion.15), kind=kLoop, calls=%fused_computation.112 | loop fusion | bytes 37453824 | tf_op jit(solution)/shard_map/slice | solution.py:46
  185.2 13.1 %fusion.8 = f32[144,128,128]{1,0,2:T(8,128)} fusion(f32[144,128,1]{1,0,2:T(8,128)S(1)} %collective-permute-done.11, f32[144,128,128]{1,0,2:T(8,128)S(1)} %fusion.15, f32[144,128,1]{1,0,2:T(8,128)S(1)} %collective-permute-done.10, f32[144,127,128]{1,0,2:T(8,128)} %get-tuple-element.11, f32[144,127,128]{1,0,2:T(8,128)} %get-tuple-element.10, ...), kind=kLoop, calls=%fused_computation.12 | loop fusion | flops 28311552 | bytes 38036608 | tf_op jit(solution)/shard_map/mul | solution.py:67
  198.3 9.6 %copy.23 = f32[144,128,128]{2,0,1:T(8,128)} copy(f32[144,128,128]{1,0,2:T(8,128)} %fusion.8) | data formatting | bytes 18874368 | tf_op jit(solution)/shard_map/mul | solution.py:67
  207.9 5.6 %all-to-all-start = ((f32[144,128,128]{2,0,1:T(8,128)}), f32[144,128,128]{2,0,1:T(8,128)}, u32[]{:S(2)}, u32[]{:S(2)}) async-start(f32[144,128,128]{2,0,1:T(8,128)} %copy.23), calls=%async_computation | async-start | bytes 18874368 | tf_op jit(solution)/shard_map/all_to_all | solution.py:80
  213.6 0.5 fusion.52
  214.2 0.1 mul.415
  214.3 0.7 copy.25
  215.0 0.4 reshape.154
  215.4 0.1 fusion.59
  215.5 2.7 fusion.50
  218.2 4.8 convolution_select_fusion
  223.0 95.8 %all-to-all-done = f32[144,128,128]{2,0,1:T(8,128)} async-done(((f32[144,128,128]{2,0,1:T(8,128)}), f32[144,128,128]{2,0,1:T(8,128)}, u32[]{:S(2)}, u32[]{:S(2)}) %all-to-all-start) | async-done | bytes 9437216 | tf_op jit(solution)/shard_map/all_to_all | solution.py:80
  318.8 6.5 %copy.24 = f32[144,8,16,128]{3,2,0,1:T(8,128)S(1)} copy(f32[144,8,16,128]{3,0,2,1:T(8,128)} %bitcast.2) | data formatting | bytes 18874368 | tf_op jit(solution)/shard_map/all_to_all | solution.py:80
  325.3 7.5 %fusion.46 = f32[16,128]{1,0:T(8,128)S(1)} fusion(f32[8,144]{1,0:T(8,128)S(1)} %mul.415, f32[144,8,16,128]{3,0,2,1:T(8,128)} %bitcast.2), kind=kLoop, calls=%fused_computation.62 | loop fusion | flops 4716544 | bytes 9449984 | tf_op jit(solution)/shard_map/reduce_sum | solution.py:103
  332.9 46.4 %fusion.3 = f32[144,8,16,128]{3,1,2,0:T(8,128)S(1)} fusion(f32[1152,1152]{1,0:T(8,128)} %convolution_select_fusion, f32[144,8,16,128]{3,2,1,0:T(8,128)S(1)} %bitcast.52, f32[2048]{0:T(1024)S(1)} %dynamic-slice_bitcast_fusion, f32[2048]{0:T(1024)S(1)} %add_divide_fusion, f32[1152]{0:T(1024)S(1)} %get-tuple-element.7, f32[2048]{0:T(1024)S(1)} %get-tuple-element.35, ...), kind=kOutput, calls=%fused_computation.6 | convolution fusion | flops 32640860160 | bytes 24233984 | tf_op jit(solution)/shard_map/dot_general | solution.py:111
  379.3 2.3 copy.28
  381.5 107.8 %all_to_all.33 = f32[1152,16,128]{2,1,0:T(8,128)S(1)} all-to-all(f32[1152,16,128]{2,1,0:T(8,128)S(1)} %bitcast.50), channel_id=1, replica_groups=mesh['sector'=4,'group'=8] {'group'}, dimensions={0} | all-to-all | bytes 18874368 | tf_op jit(solution)/shard_map/all_to_all | solution.py:113
  489.3 5.2 %copy.26 = f32[8,144,16,128]{3,2,0,1:T(8,128)} copy(f32[8,144,16,128]{3,2,1,0:T(8,128)S(1)} %bitcast.51) | data formatting | bytes 18874368 | tf_op jit(solution)/shard_map/all_to_all | solution.py:113
  (56 shorter events, 0.4 us)
Async XLA Ops:
  0.0 30.1 %copy-start = (f32[32]{0:T(128)S(1)}, f32[32]{0:T(128)}, u32[]{:S(2)}) copy-start(f32[32]{0:T(128)} %param.13) | copy-start | bytes 388
  10.5 20.3 %collective-permute-start = (f32[144,128,1]{1,0,2:T(8,128)S(1)}, f32[144,128,1]{1,0,2:T(8,128)S(1)}, u32[]{:S(2)}, u32[]{:S(2)}) collective-permute-start(f32[144,128,1]{1,0,2:T(8,128)S(1)} %get-tuple-element.32), channel_id=1, source_target_pairs={{0,8},{8,16},{16,24},{24,0},{1,9},{9,17},{17,25},{25,1},{2,10},{10... | collective-permute-start | bytes 221192 | tf_op jit(solution)/shard_map/ppermute | solution.py:20
  13.6 17.2 %collective-permute-start.1 = (f32[144,128,1]{1,0,2:T(8,128)S(1)}, f32[144,128,1]{1,0,2:T(8,128)S(1)}, u32[]{:S(2)}, u32[]{:S(2)}) collective-permute-start(f32[144,128,1]{1,0,2:T(8,128)S(1)} %get-tuple-element.33), channel_id=1, source_target_pairs={{8,0},{16,8},{24,16},{0,24},{9,1},{17,9},{25,17},{1,25},{10,2},{18... | collective-permute-start | bytes 221192 | tf_op jit(solution)/shard_map/ppermute | solution.py:22
  15.8 14.3 %copy-start.4 = (s32[1152]{0:T(1024)S(1)}, s32[1152]{0:T(1024)}, u32[]{:S(2)}) copy-start(s32[1152]{0:T(1024)} %param.12) | copy-start | bytes 13828
  15.8 14.9 %copy-start.3 = (s32[128,128]{1,0:T(8,128)S(1)}, s32[128,128]{1,0:T(8,128)}, u32[]{:S(2)}) copy-start(s32[128,128]{1,0:T(8,128)} %param.10) | copy-start | bytes 196612
  47.2 12.0 %collective-permute-start.2 = (f32[144,128,1]{1,0,2:T(8,128)S(1)}, f32[144,128,1]{1,0,2:T(8,128)S(1)}, u32[]{:S(2)}, u32[]{:S(2)}) collective-permute-start(f32[144,128,1]{1,0,2:T(8,128)S(1)} %get-tuple-element.28), channel_id=1, source_target_pairs={{0,8},{8,16},{16,24},{24,0},{1,9},{9,17},{17,25},{25,1},{2,10},{10... | collective-permute-start | bytes 221192 | tf_op jit(solution)/shard_map/ppermute | solution.py:20
  47.3 11.9 %collective-permute-start.3 = (f32[144,128,1]{1,0,2:T(8,128)S(1)}, f32[144,128,1]{1,0,2:T(8,128)S(1)}, u32[]{:S(2)}, u32[]{:S(2)}) collective-permute-start(f32[144,128,1]{1,0,2:T(8,128)S(1)} %get-tuple-element.29), channel_id=1, source_target_pairs={{8,0},{16,8},{24,16},{0,24},{9,1},{17,9},{25,17},{1,25},{10,2},{18... | collective-permute-start | bytes 221192 | tf_op jit(solution)/shard_map/ppermute | solution.py:22
  73.3 18.3 %collective-permute-start.4 = (f32[144,128,1]{1,0,2:T(8,128)S(1)}, f32[144,128,1]{1,0,2:T(8,128)S(1)}, u32[]{:S(2)}, u32[]{:S(2)}) collective-permute-start(f32[144,128,1]{1,0,2:T(8,128)S(1)} %get-tuple-element.24), channel_id=1, source_target_pairs={{0,8},{8,16},{16,24},{24,0},{1,9},{9,17},{17,25},{25,1},{2,10},{10... | collective-permute-start | bytes 221192 | tf_op jit(solution)/shard_map/ppermute | solution.py:20
  73.4 18.2 %slice-start = ((s8[9437184]{0:T(1024)(128)(4,1)}), s8[4194304]{0:T(1024)(128)(4,1)S(1)}, s32[]{:S(2)}) async-start(s8[9437184]{0:T(1024)(128)(4,1)} %bitcast.46), calls=%async_computation.2 | async-start | bytes 8388608
  73.4 18.2 %slice-start.1 = ((s8[9437184]{0:T(1024)(128)(4,1)}), s8[4194304]{0:T(1024)(128)(4,1)S(1)}, s32[]{:S(2)}) async-start(s8[9437184]{0:T(1024)(128)(4,1)} %bitcast.46), calls=%async_computation.3 | async-start | bytes 8388608
  73.4 18.2 %slice-start.2 = ((s8[9437184]{0:T(1024)(128)(4,1)}), s8[1048576]{0:T(1024)(128)(4,1)S(1)}, s32[]{:S(2)}) async-start(s8[9437184]{0:T(1024)(128)(4,1)} %bitcast.46), calls=%async_computation.4 | async-start | bytes 2097152
  73.4 18.2 %collective-permute-start.5 = (f32[144,128,1]{1,0,2:T(8,128)S(1)}, f32[144,128,1]{1,0,2:T(8,128)S(1)}, u32[]{:S(2)}, u32[]{:S(2)}) collective-permute-start(f32[144,128,1]{1,0,2:T(8,128)S(1)} %get-tuple-element.25), channel_id=1, source_target_pairs={{8,0},{16,8},{24,16},{0,24},{9,1},{17,9},{25,17},{1,25},{10,2},{18... | collective-permute-start | bytes 221192 | tf_op jit(solution)/shard_map/ppermute | solution.py:22
  105.8 18.5 %collective-permute-start.6 = (f32[144,128,1]{1,0,2:T(8,128)S(1)}, f32[144,128,1]{1,0,2:T(8,128)S(1)}, u32[]{:S(2)}, u32[]{:S(2)}) collective-permute-start(f32[144,128,1]{1,0,2:T(8,128)S(1)} %get-tuple-element.20), channel_id=1, source_target_pairs={{0,8},{8,16},{16,24},{24,0},{1,9},{9,17},{17,25},{25,1},{2,10},{10... | collective-permute-start | bytes 221192 | tf_op jit(solution)/shard_map/ppermute | solution.py:20
  105.9 18.4 %slice-start.3 = ((s8[9437184]{0:T(1024)(128)(4,1)}), s8[4194304]{0:T(1024)(128)(4,1)S(1)}, s32[]{:S(2)}) async-start(s8[9437184]{0:T(1024)(128)(4,1)} %bitcast.48), calls=%async_computation.5 | async-start | bytes 8388608
  105.9 18.4 %slice-start.4 = ((s8[9437184]{0:T(1024)(128)(4,1)}), s8[4194304]{0:T(1024)(128)(4,1)S(1)}, s32[]{:S(2)}) async-start(s8[9437184]{0:T(1024)(128)(4,1)} %bitcast.48), calls=%async_computation.6 | async-start | bytes 8388608
  105.9 18.4 %slice-start.5 = ((s8[9437184]{0:T(1024)(128)(4,1)}), s8[1048576]{0:T(1024)(128)(4,1)S(1)}, s32[]{:S(2)}) async-start(s8[9437184]{0:T(1024)(128)(4,1)} %bitcast.48), calls=%async_computation.7 | async-start | bytes 2097152
  105.9 18.4 %collective-permute-start.7 = (f32[144,128,1]{1,0,2:T(8,128)S(1)}, f32[144,128,1]{1,0,2:T(8,128)S(1)}, u32[]{:S(2)}, u32[]{:S(2)}) collective-permute-start(f32[144,128,1]{1,0,2:T(8,128)S(1)} %get-tuple-element.21), channel_id=1, source_target_pairs={{8,0},{16,8},{24,16},{0,24},{9,1},{17,9},{25,17},{1,25},{10,2},{18... | collective-permute-start | bytes 221192 | tf_op jit(solution)/shard_map/ppermute | solution.py:22
  138.5 18.3 %collective-permute-start.8 = (f32[144,128,1]{1,0,2:T(8,128)S(1)}, f32[144,128,1]{1,0,2:T(8,128)S(1)}, u32[]{:S(2)}, u32[]{:S(2)}) collective-permute-start(f32[144,128,1]{1,0,2:T(8,128)S(1)} %get-tuple-element.16), channel_id=1, source_target_pairs={{0,8},{8,16},{16,24},{24,0},{1,9},{9,17},{17,25},{25,1},{2,10},{10... | collective-permute-start | bytes 221192 | tf_op jit(solution)/shard_map/ppermute | solution.py:20
  138.5 18.2 %collective-permute-start.9 = (f32[144,128,1]{1,0,2:T(8,128)S(1)}, f32[144,128,1]{1,0,2:T(8,128)S(1)}, u32[]{:S(2)}, u32[]{:S(2)}) collective-permute-start(f32[144,128,1]{1,0,2:T(8,128)S(1)} %get-tuple-element.17), channel_id=1, source_target_pairs={{8,0},{16,8},{24,16},{0,24},{9,1},{17,9},{25,17},{1,25},{10,2},{18... | collective-permute-start | bytes 221192 | tf_op jit(solution)/shard_map/ppermute | solution.py:22
  173.2 12.0 %collective-permute-start.10 = (f32[144,128,1]{1,0,2:T(8,128)S(1)}, f32[144,128,1]{1,0,2:T(8,128)S(1)}, u32[]{:S(2)}, u32[]{:S(2)}) collective-permute-start(f32[144,128,1]{1,0,2:T(8,128)S(1)} %get-tuple-element.12), channel_id=1, source_target_pairs={{0,8},{8,16},{16,24},{24,0},{1,9},{9,17},{17,25},{25,1},{2,10},{10... | collective-permute-start | bytes 221192 | tf_op jit(solution)/shard_map/ppermute | solution.py:20
  173.2 11.9 %collective-permute-start.11 = (f32[144,128,1]{1,0,2:T(8,128)S(1)}, f32[144,128,1]{1,0,2:T(8,128)S(1)}, u32[]{:S(2)}, u32[]{:S(2)}) collective-permute-start(f32[144,128,1]{1,0,2:T(8,128)S(1)} %get-tuple-element.13), channel_id=1, source_target_pairs={{8,0},{16,8},{24,16},{0,24},{9,1},{17,9},{25,17},{1,25},{10,2},{18... | collective-permute-start | bytes 221192 | tf_op jit(solution)/shard_map/ppermute | solution.py:22
  207.9 5.7 %copy-start.6 = (f32[32]{0:T(128)S(1)}, f32[32]{0:T(128)}, u32[]{:S(2)}) copy-start(f32[32]{0:T(128)} %param.16) | copy-start | bytes 388
  207.9 5.7 %copy-start.7 = (f32[32]{0:T(128)S(1)}, f32[32]{0:T(128)}, u32[]{:S(2)}) copy-start(f32[32]{0:T(128)} %param.15) | copy-start | bytes 388
  207.9 5.7 %copy-start.8 = (f32[32]{0:T(128)S(1)}, f32[32]{0:T(128)}, u32[]{:S(2)}) copy-start(f32[32]{0:T(128)} %param.14) | copy-start | bytes 388
  207.9 6.3 %copy-start.2 = (f32[32,36,36]{2,0,1:T(8,128)S(1)}, f32[32,36,36]{2,0,1:T(8,128)}, u32[]{:S(2)}) copy-start(f32[32,36,36]{2,0,1:T(8,128)} %param.17) | copy-start | bytes 497668
  207.9 7.5 %copy-start.5 = (f32[2,16,128]{2,1,0:T(8,128)S(1)}, f32[2,16,128]{2,1,0:T(8,128)}, u32[]{:S(2)}) copy-start(f32[2,16,128]{2,1,0:T(8,128)} %param.11) | copy-start | bytes 49156
  207.9 110.9 %all-to-all-start = ((f32[144,128,128]{2,0,1:T(8,128)}), f32[144,128,128]{2,0,1:T(8,128)}, u32[]{:S(2)}, u32[]{:S(2)}) async-start(f32[144,128,128]{2,0,1:T(8,128)} %copy.23), calls=%async_computation | async-start | bytes 18874368 | tf_op jit(solution)/shard_map/all_to_all | solution.py:80
  489.3 5.2 %copy-start.1 = (f32[32]{0:T(128)S(1)}, f32[32]{0:T(128)}, u32[]{:S(2)}) copy-start(f32[32]{0:T(128)} %param.13) | copy-start | bytes 388
where the time goes:
time: 503 us; the launch traced here: 495 us
  local copies, waits for them, and re-layouts  112 us (22%)
  blocking collectives  108 us (21%)
  waiting for transfers between devices  95.8 us (19%)
  other arithmetic  93.6 us (19%)
  matrix products  54.6 us (11%)
  starting transfers between devices  30.3 us (6%)
    all_to_all x1, blocking collectives, local(): lax.all_to_all(renewed.reshape(all_comps, rows_dev, lon_local), 'group',...  108 us
    all_to_all x1, waiting for transfers between devices, local(): lax.all_to_all(propagate(spectrum, flow_x, flow_y, sea_mask), 'group', sp...  95.8 us
    mul x6, other arithmetic, propagate(): combine(wave, padded[:, :, :-2], padded[:, :, 2:], rates) * sea_mask[None]  85.5 us
    slice x6, local copies, waits for them, and re-layouts, combine(): from_south = jnp.pad(centre[:, :-1], ((0, 0), (1, 0), (0, 0)))  73.7 us
    dot_general x1, matrix products, local(): mixed = jnp.dot(coupling, energy, precision=lax.Precision.HIGHEST)  46.4 us
    ppermute x6, starting transfers between devices, extended(): lax.ppermute(head, axis, [((i + 1) % count, i) for i in range(count)])  21.2 us
    unnamed x33, local copies, waits for them, and re-layouts  12.7 us
  transfers between devices with their start and end apart: 13, of which 1 were waited for; matrix products, arithmetic and copies ran while one was open for 17% of the time, Pallas kernels for 0%

commit v1 on v0

--- a/solution.py
+++ b/solution.py
@@ -8,6 +8,17 @@
 FREQ = 32
 SUBSTEPS = 6
 LAT = 128
+
+
+def cut_along(shard, dim, size):
+    before, after = (shard.shape[:dim], shard.shape[dim + 1 :])
+    return jnp.moveaxis(shard.reshape(*before, size, -1, *after), dim, 0)
+
+
+def in_order(tiles, dim):
+    tiles = jnp.moveaxis(tiles, 0, dim)
+    lengths = tiles.shape
+    return tiles.reshape(*lengths[:dim], lengths[dim] * lengths[dim + 1], *lengths[dim + 2 :])
 
 
 def extended(cells, sides, width):
@@ -77,13 +88,15 @@
     sea_mask = land_mask.astype(jnp.float32)
     kinds = lax.dynamic_slice_in_dim(assignment, member * comps_dev, comps_dev, 0)
     flow_x, flow_y = flow_terms(kinds, courant)
-    moved = lax.all_to_all(
-        propagate(spectrum, flow_x, flow_y, sea_mask),
-        "group",
-        split_axis=1,
-        concat_axis=0,
-        tiled=True,
-    )
+    x = propagate(spectrum, flow_x, flow_y, sea_mask)
+    size, mine = (lax.axis_size("group"), lax.axis_index("group"))
+    blocks = cut_along(x, 1, size)
+    outs = [blocks[mine]]
+    for step in range(1, size):
+        sent = blocks[mine ^ step]
+        outs.append(lax.ppermute(sent, "group", [(i_2, i_2 ^ step) for i_2 in range(size)]))
+    blocks = jnp.stack(outs)[mine ^ jnp.arange(size)]
+    moved = in_order(blocks, 0)
     points = rows_dev * lon_local
     energy = moved.reshape(all_comps, points)
     sea_rows = lax.dynamic_slice_in_dim(sea_mask, member * rows_dev, rows_dev, 0).reshape(points)

time: 503 us -> 807 us (1.60)
  local copies, waits for them, and re-layouts: 112 us -> 346 us
  other arithmetic: 93.6 us -> 172 us
    slice x6 -> x11, local copies, waits for them, and re-layouts: 3.74 us -> 118 us  [extended(): lax.slice_in_dim(cells, cells.shape[dim] - width, cells.shape[dim], axis=...]
    all_to_all x1 -> x0, waiting for transfers between devices: 95.8 us -> none  [local(): lax.all_to_all(propagate(spectrum, flow_x, flow_y, sea_mask), 'group', sp...]
    ppermute x0 -> x7, waiting for transfers between devices: none -> 89.8 us  [local(): lax.ppermute(sent, 'group', [(i_2, i_2 ^ step) for i_2 in range(size)])]
    mul x6, other arithmetic: 85.5 us -> 165 us  [propagate(): combine(wave, padded[:, :, :-2], padded[:, :, 2:], rates) * sea_mask[None]]
    ppermute x0 -> x12, local copies, waits for them, and re-layouts: none -> 61.5 us  [the longest x6 31 us: extended(): lax.ppermute(tail, axis, [(i, (i + 1) % count) for i in range(count)])]
    slice x0 -> x5, local copies, waits for them, and re-layouts: none -> 29 us  [extended(): head = lax.slice_in_dim(cells, 0, width, axis=dim)]
    slice x6, local copies, waits for them, and re-layouts: 73.7 us -> 87.8 us  [combine(): from_south = jnp.pad(centre[:, :-1], ((0, 0), (1, 0), (0, 0)))]
    unnamed x33 -> x49, local copies, waits for them, and re-layouts: 12.7 us -> 24 us
  transfers between devices with their start and end apart: 13 -> 19, of which waited for: 1 -> 3; matrix products, arithmetic and copies ran while one was open for 17% -> 22% of each run, Pallas kernels for 0% -> 0%
where the time goes in v1:
time: 807 us; the launch traced here: 804 us
  local copies, waits for them, and re-layouts  346 us (43%)
  other arithmetic  172 us (21%)
  blocking collectives  109 us (14%)
  waiting for transfers between devices  89.8 us (11%)
  matrix products  52.3 us (6%)
  starting transfers between devices  33.3 us (4%)
    mul x6, other arithmetic, propagate(): combine(wave, padded[:, :, :-2], padded[:, :, 2:], rates) * sea_mask[None]  165 us
    slice x11, local copies, waits for them, and re-layouts, extended(): lax.slice_in_dim(cells, cells.shape[dim] - width, cells.shape[dim], axis=...  118 us
    all_to_all x1, blocking collectives, local(): lax.all_to_all(renewed.reshape(all_comps, rows_dev, lon_local), 'group',...  109 us
    ppermute x7, waiting for transfers between devices, local(): lax.ppermute(sent, 'group', [(i_2, i_2 ^ step) for i_2 in range(size)])  89.8 us
    slice x6, local copies, waits for them, and re-layouts, combine(): from_south = jnp.pad(centre[:, :-1], ((0, 0), (1, 0), (0, 0)))  87.8 us
    dot_general x1, matrix products, local(): mixed = jnp.dot(coupling, energy, precision=lax.Precision.HIGHEST)  44.2 us
    ppermute x6, local copies, waits for them, and re-layouts, extended(): lax.ppermute(tail, axis, [(i, (i + 1) % count) for i in range(count)])  31 us
    ppermute x6, local copies, waits for them, and re-layouts, extended(): lax.ppermute(head, axis, [((i + 1) % count, i) for i in range(count)])  30.5 us
  transfers between devices with their start and end apart: 19, of which 3 were waited for; matrix products, arithmetic and copies ran while one was open for 22% of the time, Pallas kernels for 0%

profile of v1, /device:TPU:0, one launch (start us, length us, event | category | flops | bytes accessed | tf_op | source)
XLA Modules:
  0.0 803.9 jit_solution(11567643149918698903)
XLA Ops:
  0.0 14.8 %fusion.83 = (f32[144,128,1]{2,1,0:T(8,128)}, f32[144,128,1]{2,1,0:T(8,128)}) fusion(f32[144,128,128]{2,1,0:T(8,128)} %param.9), kind=kLoop, calls=%fused_computation.141 | loop fusion | bytes 294912 | tf_op jit(solution)/shard_map/slice | solution.py:28
  14.8 5.8 copy.49
  23.8 5.8 copy.50
  31.9 14.7 %fusion.82 = (f32[144,127,128]{2,1,0:T(8,128)}, f32[144,127,128]{2,1,0:T(8,128)}) fusion(f32[144,128,128]{2,1,0:T(8,128)} %param.9), kind=kLoop, calls=%fused_computation.140 | loop fusion | bytes 37453824 | tf_op jit(solution)/shard_map/slice | solution.py:57
  56.0 5.2 copy.24
  61.2 5.1 copy.26
  66.3 27.0 %fusion.43 = f32[144,128,128]{2,1,0:T(8,128)} fusion(f32[144,128,1]{2,1,0:T(8,128)} %copy.26, f32[144,128,128]{2,1,0:T(8,128)} %param.9, f32[144,128,1]{2,1,0:T(8,128)} %copy.24, f32[144,127,128]{2,1,0:T(8,128)} %get-tuple-element.38, f32[144,127,128]{2,1,0:T(8,128)} %get-tuple-element.37, f32[128,128]{1,0:T(8,128)S(1)} %convert_element_type.37, ...), kind=kLoop, calls=%fused_computation.58 | loop fusion | flops 28311552 | bytes 38036608 | tf_op jit(solution)/shard_map/mul | solution.py:78
  93.3 15.0 %fusion.81 = (f32[144,128,1]{2,1,0:T(8,128)}, f32[144,128,1]{2,1,0:T(8,128)}) fusion(f32[144,128,128]{2,1,0:T(8,128)} %fusion.43), kind=kLoop, calls=%fused_computation.139 | loop fusion | bytes 294912 | tf_op jit(solution)/shard_map/slice | solution.py:28
  108.3 5.8 copy.27
  114.1 5.8 copy.29
  124.0 14.7 %fusion.80 = (f32[144,127,128]{2,1,0:T(8,128)}, f32[144,127,128]{2,1,0:T(8,128)}) fusion(f32[144,128,128]{2,1,0:T(8,128)} %fusion.43), kind=kLoop, calls=%fused_computation.138 | loop fusion | bytes 37453824 | tf_op jit(solution)/shard_map/slice | solution.py:57
  138.7 5.2 copy.28
  143.8 5.1 copy.30
  148.9 27.9 %fusion.36 = f32[144,128,128]{2,1,0:T(8,128)} fusion(f32[144,128,1]{2,1,0:T(8,128)} %copy.30, f32[144,128,128]{2,1,0:T(8,128)} %fusion.43, f32[144,128,1]{2,1,0:T(8,128)} %copy.28, f32[144,127,128]{2,1,0:T(8,128)} %get-tuple-element.34, f32[144,127,128]{2,1,0:T(8,128)} %get-tuple-element.33, f32[128,128]{1,0:T(8,128)S(1)} %convert_element_type.37, ...), kind=kLoop, calls=%fused_computation.49 | loop fusion | flops 28311552 | bytes 38036608 | tf_op jit(solution)/shard_map/mul | solution.py:78
  176.8 14.8 %fusion.79 = (f32[144,128,1]{2,1,0:T(8,128)}, f32[144,128,1]{2,1,0:T(8,128)}) fusion(f32[144,128,128]{2,1,0:T(8,128)} %fusion.36), kind=kLoop, calls=%fused_computation.137 | loop fusion | bytes 294912 | tf_op jit(solution)/shard_map/slice | solution.py:28
  191.6 5.8 copy.31
  197.5 5.8 copy.33
  207.2 14.5 %fusion.78 = (f32[144,127,128]{2,1,0:T(8,128)}, f32[144,127,128]{2,1,0:T(8,128)}) fusion(f32[144,128,128]{2,1,0:T(8,128)} %fusion.36), kind=kLoop, calls=%fused_computation.136 | loop fusion | bytes 37453824 | tf_op jit(solution)/shard_map/slice | solution.py:57
  221.7 5.2 copy.32
  231.9 27.2 %fusion.29 = f32[144,128,128]{2,1,0:T(8,128)} fusion(f32[144,128,1]{2,1,0:T(8,128)} %copy.34, f32[144,128,128]{2,1,0:T(8,128)} %fusion.36, f32[144,128,1]{2,1,0:T(8,128)} %copy.32, f32[144,127,128]{2,1,0:T(8,128)} %get-tuple-element.30, f32[144,127,128]{2,1,0:T(8,128)} %get-tuple-element.29, f32[128,128]{1,0:T(8,128)S(1)} %convert_element_type.37, ...), kind=kLoop, calls=%fused_computation.40 | loop fusion | flops 28311552 | bytes 38036608 | tf_op jit(solution)/shard_map/mul | solution.py:78
  259.1 15.0 %fusion.77 = (f32[144,128,1]{2,1,0:T(8,128)}, f32[144,128,1]{2,1,0:T(8,128)}) fusion(f32[144,128,128]{2,1,0:T(8,128)} %fusion.29), kind=kLoop, calls=%fused_computation.135 | loop fusion | bytes 294912 | tf_op jit(solution)/shard_map/slice | solution.py:28
  274.1 5.8 copy.35
  279.9 5.8 copy.37
  290.0 14.7 %fusion.76 = (f32[144,127,128]{2,1,0:T(8,128)}, f32[144,127,128]{2,1,0:T(8,128)}) fusion(f32[144,128,128]{2,1,0:T(8,128)} %fusion.29), kind=kLoop, calls=%fused_computation.134 | loop fusion | bytes 37453824 | tf_op jit(solution)/shard_map/slice | solution.py:57
  304.7 5.2 copy.36
  309.8 5.1 copy.38
  314.9 27.9 %fusion.22 = f32[144,128,128]{2,1,0:T(8,128)} fusion(f32[144,128,1]{2,1,0:T(8,128)} %copy.38, f32[144,128,128]{2,1,0:T(8,128)} %fusion.29, f32[144,128,1]{2,1,0:T(8,128)} %copy.36, f32[144,127,128]{2,1,0:T(8,128)} %get-tuple-element.26, f32[144,127,128]{2,1,0:T(8,128)} %get-tuple-element.25, f32[128,128]{1,0:T(8,128)S(1)} %convert_element_type.37, ...), kind=kLoop, calls=%fused_computation.31 | loop fusion | flops 28311552 | bytes 38036608 | tf_op jit(solution)/shard_map/mul | solution.py:78
  342.8 14.8 %fusion.75 = (f32[144,128,1]{2,1,0:T(8,128)}, f32[144,128,1]{2,1,0:T(8,128)}) fusion(f32[144,128,128]{2,1,0:T(8,128)} %fusion.22), kind=kLoop, calls=%fused_computation.133 | loop fusion | bytes 294912 | tf_op jit(solution)/shard_map/slice | solution.py:28
  357.6 5.8 copy.39
  363.5 5.8 copy.41
  373.2 14.5 %fusion.74 = (f32[144,127,128]{2,1,0:T(8,128)}, f32[144,127,128]{2,1,0:T(8,128)}) fusion(f32[144,128,128]{2,1,0:T(8,128)} %fusion.22), kind=kLoop, calls=%fused_computation.132 | loop fusion | bytes 37453824 | tf_op jit(solution)/shard_map/slice | solution.py:57
  387.7 5.2 copy.40
  397.9 27.2 %fusion.15 = f32[144,128,128]{2,1,0:T(8,128)} fusion(f32[144,128,1]{2,1,0:T(8,128)} %copy.42, f32[144,128,128]{2,1,0:T(8,128)} %fusion.22, f32[144,128,1]{2,1,0:T(8,128)} %copy.40, f32[144,127,128]{2,1,0:T(8,128)} %get-tuple-element.22, f32[144,127,128]{2,1,0:T(8,128)} %get-tuple-element.21, f32[128,128]{1,0:T(8,128)S(1)} %convert_element_type.37, ...), kind=kLoop, calls=%fused_computation.22 | loop fusion | flops 28311552 | bytes 38036608 | tf_op jit(solution)/shard_map/mul | solution.py:78
  425.1 15.0 %fusion.73 = (f32[144,128,1]{2,1,0:T(8,128)}, f32[144,128,1]{2,1,0:T(8,128)}) fusion(f32[144,128,128]{2,1,0:T(8,128)} %fusion.15), kind=kLoop, calls=%fused_computation.131 | loop fusion | bytes 294912 | tf_op jit(solution)/shard_map/slice | solution.py:28
  440.1 5.8 copy.43
  445.9 5.8 copy.45
  455.8 14.7 %fusion.72 = (f32[144,127,128]{2,1,0:T(8,128)}, f32[144,127,128]{2,1,0:T(8,128)}) fusion(f32[144,128,128]{2,1,0:T(8,128)} %fusion.15), kind=kLoop, calls=%fused_computation.130 | loop fusion | bytes 37453824 | tf_op jit(solution)/shard_map/slice | solution.py:57
  470.4 5.2 copy.44
  480.7 27.9 %fusion.8 = f32[144,128,128]{2,1,0:T(8,128)} fusion(f32[144,128,1]{2,1,0:T(8,128)} %copy.46, f32[144,128,128]{2,1,0:T(8,128)} %fusion.15, f32[144,128,1]{2,1,0:T(8,128)} %copy.44, f32[144,127,128]{2,1,0:T(8,128)} %get-tuple-element.18, f32[144,127,128]{2,1,0:T(8,128)} %get-tuple-element.17, f32[128,128]{1,0:T(8,128)S(1)} %convert_element_type.37, ...), kind=kLoop, calls=%fused_computation.13 | loop fusion | flops 28311552 | bytes 38036608 | tf_op jit(solution)/shard_map/mul | solution.py:78
  508.6 6.8 dynamic-slice_bitcast_fusion
  530.2 15.5 %collective-permute-done.13 = f32[144,16,128]{2,1,0:T(8,128)S(1)} collective-permute-done((f32[144,16,128]{2,1,0:T(8,128)}, f32[144,16,128]{2,1,0:T(8,128)S(1)}, u32[]{:S(2)}, u32[]{:S(2)}) %collective-permute-start.13) | collective-permute-done | bytes 1179680 | tf_op jit(solution)/shard_map/ppermute | solution.py:97
  548.2 22.1 %collective-permute-done.14 = f32[144,16,128]{2,1,0:T(8,128)S(1)} collective-permute-done((f32[144,16,128]{2,1,0:T(8,128)}, f32[144,16,128]{2,1,0:T(8,128)S(1)}, u32[]{:S(2)}, u32[]{:S(2)}) %collective-permute-start.14) | collective-permute-done | bytes 1179680 | tf_op jit(solution)/shard_map/ppermute | solution.py:97
  572.4 52.2 %collective-permute-done.16 = f32[144,16,128]{2,1,0:T(8,128)S(1)} collective-permute-done((f32[144,16,128]{2,1,0:T(8,128)}, f32[144,16,128]{2,1,0:T(8,128)S(1)}, u32[]{:S(2)}, u32[]{:S(2)}) %collective-permute-start.16) | collective-permute-done | bytes 1179680 | tf_op jit(solution)/shard_map/ppermute | solution.py:97
  627.9 8.5 %gather_fusion = f32[8,144,16,128]{3,2,1,0:T(8,128)} fusion(f32[8,144,16,128]{3,2,1,0:T(8,128)} %bitcast_dynamic-update-slice_fusion, s32[1024]{0:T(1024)S(1)} %pad_clamp_fusion), kind=kCustom, calls=%fused_computation | custom fusion | bytes 18874400 | tf_op jit(solution)/shard_map/gather | solution.py:98
  636.5 5.9 multiply_reduce_fusion
  642.9 44.2 %fusion.3 = f32[144,8,16,128]{3,1,2,0:T(8,128)S(1)} fusion(f32[1152,1152]{1,0:T(8,128)} %convolution_select_fusion, f32[144,8,16,128]{3,2,1,0:T(8,128)S(1)} %bitcast.76, f32[2048]{0:T(1024)S(1)} %copy-done.14, f32[2048]{0:T(1024)S(1)} %add_divide_fusion, f32[1152]{0:T(1024)S(1)} %copy-done.11, f32[2048]{0:T(1024)S(1)} %copy-done.15, ...), kind=kOutput, calls=%fused_computation.7 | convolution fusion | flops 32640860160 | bytes 24233984 | tf_op jit(solution)/shard_map/dot_general | solution.py:124
  689.4 109.0 %all_to_all.18 = f32[1152,16,128]{2,1,0:T(8,128)S(1)} all-to-all(f32[1152,16,128]{2,1,0:T(8,128)S(1)} %bitcast.77), channel_id=1, replica_groups=mesh['sector'=4,'group'=8] {'group'}, dimensions={0} | all-to-all | bytes 18874368 | tf_op jit(solution)/shard_map/all_to_all | solution.py:126
  798.4 5.2 copy.48
  (106 shorter events, 75.7 us)
Async XLA Ops:
  0.0 46.8 %copy-start = (f32[32]{0:T(128)S(1)}, f32[32]{0:T(128)}, u32[]{:S(2)}) copy-start(f32[32]{0:T(128)} %param.13) | copy-start | bytes 388
  20.6 35.3 %collective-permute-start = (f32[144,128,1]{1,0,2:T(8,128)S(1)}, f32[144,128,1]{1,0,2:T(8,128)S(1)}, u32[]{:S(2)}, u32[]{:S(2)}) collective-permute-start(f32[144,128,1]{1,0,2:T(8,128)S(1)} %copy.49), channel_id=1, source_target_pairs={{0,8},{8,16},{16,24},{24,0},{1,9},{9,17},{17,25},{25,1},{2,10},{10... | collective-permute-start | bytes 221192 | tf_op jit(solution)/shard_map/ppermute | solution.py:31
  29.6 31.6 %collective-permute-start.1 = (f32[144,128,1]{1,0,2:T(8,128)S(1)}, f32[144,128,1]{1,0,2:T(8,128)S(1)}, u32[]{:S(2)}, u32[]{:S(2)}) collective-permute-start(f32[144,128,1]{1,0,2:T(8,128)S(1)} %copy.50), channel_id=1, source_target_pairs={{8,0},{16,8},{24,16},{0,24},{9,1},{17,9},{25,17},{1,25},{10,2},{18... | collective-permute-start | bytes 221192 | tf_op jit(solution)/shard_map/ppermute | solution.py:33
  31.9 14.8 %copy-start.7 = (s32[1152]{0:T(1024)S(1)}, s32[1152]{0:T(1024)}, u32[]{:S(2)}) copy-start(s32[1152]{0:T(1024)} %param.12) | copy-start | bytes 13828
  31.9 15.3 %copy-start.3 = (f32[32,36,36]{2,0,1:T(8,128)S(1)}, f32[32,36,36]{2,0,1:T(8,128)}, u32[]{:S(2)}) copy-start(f32[32,36,36]{2,0,1:T(8,128)} %param.17) | copy-start | bytes 497668
  46.6 9.3 %copy-start.6 = (s32[128,128]{1,0:T(8,128)S(1)}, s32[128,128]{1,0:T(8,128)}, u32[]{:S(2)}) copy-start(s32[128,128]{1,0:T(8,128)} %param.10) | copy-start | bytes 196612
  46.7 14.5 %copy-start.4 = (s32[1152]{0:T(1024)}, s32[1152]{0:T(1024)S(1)}, u32[]{:S(2)}) copy-start(s32[1152]{0:T(1024)S(1)} %get-tuple-element.46) | copy-start | bytes 13828
  114.1 24.6 %collective-permute-start.2 = (f32[144,128,1]{1,0,2:T(8,128)S(1)}, f32[144,128,1]{1,0,2:T(8,128)S(1)}, u32[]{:S(2)}, u32[]{:S(2)}) collective-permute-start(f32[144,128,1]{1,0,2:T(8,128)S(1)} %copy.27), channel_id=1, source_target_pairs={{0,8},{8,16},{16,24},{24,0},{1,9},{9,17},{17,25},{25,1},{2,10},{10... | collective-permute-start | bytes 221192 | tf_op jit(solution)/shard_map/ppermute | solution.py:31
  120.0 23.9 %collective-permute-start.3 = (f32[144,128,1]{1,0,2:T(8,128)S(1)}, f32[144,128,1]{1,0,2:T(8,128)S(1)}, u32[]{:S(2)}, u32[]{:S(2)}) collective-permute-start(f32[144,128,1]{1,0,2:T(8,128)S(1)} %copy.29), channel_id=1, source_target_pairs={{8,0},{16,8},{24,16},{0,24},{9,1},{17,9},{25,17},{1,25},{10,2},{18... | collective-permute-start | bytes 221192 | tf_op jit(solution)/shard_map/ppermute | solution.py:33
  197.4 24.3 %collective-permute-start.4 = (f32[144,128,1]{1,0,2:T(8,128)S(1)}, f32[144,128,1]{1,0,2:T(8,128)S(1)}, u32[]{:S(2)}, u32[]{:S(2)}) collective-permute-start(f32[144,128,1]{1,0,2:T(8,128)S(1)} %copy.31), channel_id=1, source_target_pairs={{0,8},{8,16},{16,24},{24,0},{1,9},{9,17},{17,25},{25,1},{2,10},{10... | collective-permute-start | bytes 221192 | tf_op jit(solution)/shard_map/ppermute | solution.py:31
  203.3 23.6 %collective-permute-start.5 = (f32[144,128,1]{1,0,2:T(8,128)S(1)}, f32[144,128,1]{1,0,2:T(8,128)S(1)}, u32[]{:S(2)}, u32[]{:S(2)}) collective-permute-start(f32[144,128,1]{1,0,2:T(8,128)S(1)} %copy.33), channel_id=1, source_target_pairs={{8,0},{16,8},{24,16},{0,24},{9,1},{17,9},{25,17},{1,25},{10,2},{18... | collective-permute-start | bytes 221192 | tf_op jit(solution)/shard_map/ppermute | solution.py:33
  279.9 24.8 %collective-permute-start.6 = (f32[144,128,1]{1,0,2:T(8,128)S(1)}, f32[144,128,1]{1,0,2:T(8,128)S(1)}, u32[]{:S(2)}, u32[]{:S(2)}) collective-permute-start(f32[144,128,1]{1,0,2:T(8,128)S(1)} %copy.35), channel_id=1, source_target_pairs={{0,8},{8,16},{16,24},{24,0},{1,9},{9,17},{17,25},{25,1},{2,10},{10... | collective-permute-start | bytes 221192 | tf_op jit(solution)/shard_map/ppermute | solution.py:31
  285.8 24.1 %collective-permute-start.7 = (f32[144,128,1]{1,0,2:T(8,128)S(1)}, f32[144,128,1]{1,0,2:T(8,128)S(1)}, u32[]{:S(2)}, u32[]{:S(2)}) collective-permute-start(f32[144,128,1]{1,0,2:T(8,128)S(1)} %copy.37), channel_id=1, source_target_pairs={{8,0},{16,8},{24,16},{0,24},{9,1},{17,9},{25,17},{1,25},{10,2},{18... | collective-permute-start | bytes 221192 | tf_op jit(solution)/shard_map/ppermute | solution.py:33
  363.4 24.3 %collective-permute-start.8 = (f32[144,128,1]{1,0,2:T(8,128)S(1)}, f32[144,128,1]{1,0,2:T(8,128)S(1)}, u32[]{:S(2)}, u32[]{:S(2)}) collective-permute-start(f32[144,128,1]{1,0,2:T(8,128)S(1)} %copy.39), channel_id=1, source_target_pairs={{0,8},{8,16},{16,24},{24,0},{1,9},{9,17},{17,25},{25,1},{2,10},{10... | collective-permute-start | bytes 221192 | tf_op jit(solution)/shard_map/ppermute | solution.py:31
  369.3 23.6 %collective-permute-start.9 = (f32[144,128,1]{1,0,2:T(8,128)S(1)}, f32[144,128,1]{1,0,2:T(8,128)S(1)}, u32[]{:S(2)}, u32[]{:S(2)}) collective-permute-start(f32[144,128,1]{1,0,2:T(8,128)S(1)} %copy.41), channel_id=1, source_target_pairs={{8,0},{16,8},{24,16},{0,24},{9,1},{17,9},{25,17},{1,25},{10,2},{18... | collective-permute-start | bytes 221192 | tf_op jit(solution)/shard_map/ppermute | solution.py:33
  445.9 24.6 %collective-permute-start.10 = (f32[144,128,1]{1,0,2:T(8,128)S(1)}, f32[144,128,1]{1,0,2:T(8,128)S(1)}, u32[]{:S(2)}, u32[]{:S(2)}) collective-permute-start(f32[144,128,1]{1,0,2:T(8,128)S(1)} %copy.43), channel_id=1, source_target_pairs={{0,8},{8,16},{16,24},{24,0},{1,9},{9,17},{17,25},{25,1},{2,10},{10... | collective-permute-start | bytes 221192 | tf_op jit(solution)/shard_map/ppermute | solution.py:31
  451.7 23.8 %collective-permute-start.11 = (f32[144,128,1]{1,0,2:T(8,128)S(1)}, f32[144,128,1]{1,0,2:T(8,128)S(1)}, u32[]{:S(2)}, u32[]{:S(2)}) collective-permute-start(f32[144,128,1]{1,0,2:T(8,128)S(1)} %copy.45), channel_id=1, source_target_pairs={{8,0},{16,8},{24,16},{0,24},{9,1},{17,9},{25,17},{1,25},{10,2},{18... | collective-permute-start | bytes 221192 | tf_op jit(solution)/shard_map/ppermute | solution.py:33
  508.6 7.5 copy-start.5
  508.6 7.5 copy-start.16
  508.6 7.4 copy-start.17
  508.6 7.4 copy-start.18
  508.6 11.8 %copy-start.8 = (s32[1152]{0:T(1024)S(1)}, s32[1152]{0:T(1024)}, u32[]{:S(2)}) copy-start(s32[1152]{0:T(1024)} %param.12) | copy-start | bytes 13828
  515.4 11.1 %collective-permute-start.12 = (f32[144,16,128]{2,1,0:T(8,128)}, f32[144,16,128]{2,1,0:T(8,128)S(1)}, u32[]{:S(2)}, u32[]{:S(2)}) collective-permute-start(f32[144,16,128]{2,1,0:T(8,128)} %get-tuple-element.16), channel_id=1, source_target_pairs={{0,1},{1,0},{2,3},{3,2},{4,5},{5,4},{6,7},{7,6},{8,9},{9,8},{10,11... | collective-permute-start | bytes 3538952 | tf_op jit(solution)/shard_map/ppermute | solution.py:97
  516.5 29.1 %collective-permute-start.13 = (f32[144,16,128]{2,1,0:T(8,128)}, f32[144,16,128]{2,1,0:T(8,128)S(1)}, u32[]{:S(2)}, u32[]{:S(2)}) collective-permute-start(f32[144,16,128]{2,1,0:T(8,128)} %get-tuple-element.15), channel_id=1, source_target_pairs={{0,2},{1,3},{2,0},{3,1},{4,6},{5,7},{6,4},{7,5},{8,10},{9,11},{10,... | collective-permute-start | bytes 3538952 | tf_op jit(solution)/shard_map/ppermute | solution.py:97
  518.9 51.3 %collective-permute-start.14 = (f32[144,16,128]{2,1,0:T(8,128)}, f32[144,16,128]{2,1,0:T(8,128)S(1)}, u32[]{:S(2)}, u32[]{:S(2)}) collective-permute-start(f32[144,16,128]{2,1,0:T(8,128)} %get-tuple-element.14), channel_id=1, source_target_pairs={{0,3},{1,2},{2,1},{3,0},{4,7},{5,6},{6,5},{7,4},{8,11},{9,10},{10,... | collective-permute-start | bytes 3538952 | tf_op jit(solution)/shard_map/ppermute | solution.py:97
  521.1 50.2 %collective-permute-start.15 = (f32[144,16,128]{2,1,0:T(8,128)}, f32[144,16,128]{2,1,0:T(8,128)S(1)}, u32[]{:S(2)}, u32[]{:S(2)}) collective-permute-start(f32[144,16,128]{2,1,0:T(8,128)} %get-tuple-element.13), channel_id=1, source_target_pairs={{0,4},{1,5},{2,6},{3,7},{4,0},{5,1},{6,2},{7,3},{8,12},{9,13},{10,... | collective-permute-start | bytes 3538952 | tf_op jit(solution)/shard_map/ppermute | solution.py:97
  524.1 100.5 %collective-permute-start.16 = (f32[144,16,128]{2,1,0:T(8,128)}, f32[144,16,128]{2,1,0:T(8,128)S(1)}, u32[]{:S(2)}, u32[]{:S(2)}) collective-permute-start(f32[144,16,128]{2,1,0:T(8,128)} %get-tuple-element.12), channel_id=1, source_target_pairs={{0,5},{1,4},{2,7},{3,6},{4,1},{5,0},{6,3},{7,2},{8,13},{9,12},{10,... | collective-permute-start | bytes 3538952 | tf_op jit(solution)/shard_map/ppermute | solution.py:97
  526.5 99.2 %collective-permute-start.17 = (f32[144,16,128]{2,1,0:T(8,128)}, f32[144,16,128]{2,1,0:T(8,128)S(1)}, u32[]{:S(2)}, u32[]{:S(2)}) collective-permute-start(f32[144,16,128]{2,1,0:T(8,128)} %get-tuple-element.11), channel_id=1, source_target_pairs={{0,6},{1,7},{2,4},{3,5},{4,2},{5,3},{6,0},{7,1},{8,14},{9,15},{10,... | collective-permute-start | bytes 3538952 | tf_op jit(solution)/shard_map/ppermute | solution.py:97
  545.6 81.2 %collective-permute-start.18 = (f32[144,16,128]{2,1,0:T(8,128)}, f32[144,16,128]{2,1,0:T(8,128)S(1)}, u32[]{:S(2)}, u32[]{:S(2)}) collective-permute-start(f32[144,16,128]{2,1,0:T(8,128)} %get-tuple-element.10), channel_id=1, source_target_pairs={{0,7},{1,6},{2,5},{3,4},{4,3},{5,2},{6,1},{7,0},{8,15},{9,14},{10,... | collective-permute-start | bytes 3538952 | tf_op jit(solution)/shard_map/ppermute | solution.py:97
  627.9 8.5 %copy-start.9 = (f32[8,144]{1,0:T(8,128)S(1)}, f32[8,144]{1,0:T(8,128)}, u32[]{:S(2)}) copy-start(f32[8,144]{1,0:T(8,128)} %mul.415) | copy-start | bytes 13828
  627.9 14.5 %copy-start.15 = (f32[2048]{0:T(1024)S(1)}, f32[2048]{0:T(1024)}, u32[]{:S(2)}) copy-start(f32[2048]{0:T(1024)} %get-tuple-element.42) | copy-start | bytes 24580
  636.4 6.4 copy-start.2
  636.4 6.4 copy-start.10
  636.4 6.4 copy-start.11
  636.4 6.4 copy-start.12
  636.4 6.4 copy-start.13
  636.4 6.4 copy-start.14
  798.4 5.2 copy-start.1
